TPU v7x, 128 devices: a whole 4x4x4 slice. The times are simulated.
128 devices in a mesh: fsdp: 4 (over z_hi, core), ctx: 32 (over z_lo, x, y).
Axes of the slice: x: 4, y: 4, z: 4 (z_hi: 2, z_lo: 2; z = z_hi * 2 + z_lo), core: 2. Of those that a mesh axis runs over, the one named last changes fastest.
Arguments:
- tokens: bfloat16 [4, 16384, 8192], P('fsdp', 'ctx'), may hold values from -56 to 56
- codes: int32 [128, 20480], P('fsdp'), may hold values from 0 to 65535
- scales: bfloat16 [128, 1280], P('fsdp'), may hold values from 0.0039978027 to 0.039794922
- down_adapter_matrix: bfloat16 [128, 4096], P('fsdp'), may hold values from -0.0625 to 0.0625
- up_adapter_matrix: bfloat16 [64, 1280], replicated, may hold values from -0.75 to 0.75
- positions: int32 [4, 16384], P('fsdp', 'ctx'), may hold values from 0 to 16383, as said below
Outputs:
- attended: bfloat16 [4, 16384, 1024], P('fsdp', 'ctx')
Inputs may be any that keep to these rules, and one draw needn't show every extreme that they name: In each sequence the first and the last 256 tokens of each device's share hold consecutive increasing positions, of some block a and of block 63 - a of the sequence (blocks of 256 positions), a different a on each device of a sequence; every position of 0 to 16383 appears once in each sequence.
All inputs are finite; a program needn't handle non-finite values.
Results may differ from a plain program's by a relative error of at most 0.014.
Values may be sent and summed in bfloat16 or wider, within the bound.
A program may use at most 192 MiB of HBM per device.

v0:
```python
import jax
import jax.numpy as jnp
from jax import lax
from jax.sharding import PartitionSpec as P

QH = 8
HD = 128


normal_float_levels = [
    -1.0,
    -0.6961928009986877,
    -0.5250730514526367,
    -0.39491748809814453,
    -0.28444138169288635,
    -0.18477343022823334,
    -0.09105003625154495,
    0.0,
    0.07958029955625534,
    0.16093020141124725,
    0.24611230194568634,
    0.33791524171829224,
    0.44070982933044434,
    0.5626170039176941,
    0.7229568362236023,
    1.0,
]
rope_base = 500000.0
adapter_scaling = 0.5


def unpack_codes(packed):
    blocks = packed.shape[0]
    words = packed.reshape(blocks, 64, -1)
    nibbles = [jnp.remainder(jnp.floor_divide(words, 16**place), 16) for place in range(4)]
    return jnp.stack(nibbles, axis=-1).reshape(blocks, 64, -1)


def pick_level(code_full):
    bit_flags = [jnp.remainder(jnp.floor_divide(code_full, 2**place), 2) == 1 for place in range(4)]
    current = [jnp.float32(level) for level in normal_float_levels]
    for place in range(4):
        current = [
            jnp.where(bit_flags[place], current[2 * pair + 1], current[2 * pair])
            for pair in range(len(current) // 2)
        ]
    return current[0]


def dequantize(packed, block_scales):
    code_full = unpack_codes(packed)
    values = pick_level(code_full)
    scaled = values * block_scales.astype(jnp.float32)[:, None, :]
    return scaled.reshape(-1, scaled.shape[-1]).astype(jnp.bfloat16)


def rotate_pairs(values, angles):
    half_size = values.shape[-1] // 2
    first_half = values[..., :half_size]
    second_half = values[..., half_size:]
    cosine = jnp.cos(angles)
    sine = jnp.sin(angles)
    return jnp.concatenate(
        [first_half * cosine - second_half * sine, second_half * cosine + first_half * sine],
        axis=-1,
    )


def make_angles(token_position):
    half_size = HD // 2
    steps_idx = jnp.arange(half_size, dtype=jnp.float32)
    inverse = jnp.exp(-jnp.log(jnp.float32(rope_base)) * 2.0 * steps_idx / HD)
    return token_position.astype(jnp.float32)[:, None] * inverse[None, :]


def tile_update(state, query_part, query_pos, tile, tile_pos):
    running_max, running_sum, running_acc = state
    scores = jnp.einsum("hqd,kd->hqk", query_part, tile[:, :HD], preferred_element_type=jnp.float32)
    scores = jnp.where(tile_pos[None, None, :] <= query_pos[None, :, None], scores, -jnp.inf)
    new_max = jnp.maximum(running_max, jnp.max(scores, axis=-1))
    factor = jnp.exp(running_max - new_max)
    expo = jnp.exp(scores - new_max[..., None])
    new_sum = running_sum * factor + jnp.sum(expo, axis=-1)
    weights = expo.astype(jnp.bfloat16)
    new_acc = running_acc * factor[..., None] + jnp.einsum(
        "hqk,kd->hqd", weights, tile[:, HD:], preferred_element_type=jnp.float32
    )
    return (new_max, new_sum, new_acc)


def on_device(tokens, codes, scales, down_adapter_matrix, up_adapter_matrix, positions):
    local_tokens = tokens[0]
    local_pos = positions[0]
    tok_count = local_tokens.shape[0]
    adapter_rank_size = up_adapter_matrix.shape[0]
    input_width = up_adapter_matrix.shape[1]
    own_weight = dequantize(codes, scales).reshape(scales.shape[0], 64 * input_width)
    weight_piece = lax.all_gather(own_weight, "fsdp", axis=0, tiled=True)
    adapter_slice = lax.all_gather(down_adapter_matrix, "fsdp", axis=0, tiled=True)
    rows = weight_piece.shape[0] * 64
    first_total = jnp.dot(
        local_tokens, weight_piece.reshape(rows, input_width), preferred_element_type=jnp.float32
    )
    second_total = jnp.dot(
        local_tokens,
        adapter_slice.reshape(rows, adapter_rank_size),
        preferred_element_type=jnp.float32,
    )
    low_rank_output = second_total.astype(jnp.bfloat16)
    joined_output = first_total + adapter_scaling * jnp.dot(
        low_rank_output, up_adapter_matrix, preferred_element_type=jnp.float32
    )
    angles = make_angles(local_pos)
    qwidth = QH * HD
    query_output = joined_output[:, :qwidth].reshape(tok_count, QH, HD).transpose(1, 0, 2)
    query_output = (rotate_pairs(query_output, angles) * HD ** (-0.5)).astype(jnp.bfloat16)
    key = rotate_pairs(joined_output[:, qwidth : qwidth + HD], angles).astype(jnp.bfloat16)
    value_output = joined_output[:, qwidth + HD :].astype(jnp.bfloat16)
    keys_values = jnp.concatenate([key, value_output], axis=1)
    all_positions = lax.all_gather(local_pos, "ctx", axis=0, tiled=True)
    half_size = tok_count // 2
    query_parts = (query_output[:, :half_size], query_output[:, half_size:])
    pos_parts = (local_pos[:half_size], local_pos[half_size:])
    empty_state = (
        jnp.full((QH, half_size), -1e30, jnp.float32),
        jnp.zeros((QH, half_size), jnp.float32),
        jnp.zeros((QH, half_size, HD), jnp.float32),
    )
    states = (empty_state, empty_state)
    piece = lax.all_gather(keys_values, "ctx", axis=0, tiled=True)
    count = piece.shape[0]

    def one_tile(carry, tile_idx):
        tile = lax.dynamic_slice_in_dim(piece, tile_idx * half_size, half_size, 0)
        tile_pos = lax.dynamic_slice_in_dim(all_positions, tile_idx * half_size, half_size, 0)
        updated = []
        for part_idx in range(2):

            def apply_tile(state, part_idx=part_idx):
                return tile_update(
                    state, query_parts[part_idx], pos_parts[part_idx], tile, tile_pos
                )

            def keep_state(state):
                return state

            visible = jnp.min(tile_pos) <= jnp.max(pos_parts[part_idx])
            updated.append(lax.cond(visible, apply_tile, keep_state, carry[part_idx]))
        return ((updated[0], updated[1]), None)

    states, unused = lax.scan(one_tile, states, jnp.arange(count // half_size, dtype=jnp.int32))
    halves = [states[part_idx][2] / states[part_idx][1][..., None] for part_idx in range(2)]
    combined = jnp.concatenate(halves, axis=1)
    attended = combined.transpose(1, 0, 2).reshape(tok_count, QH * HD).astype(jnp.bfloat16)
    return attended[None]


def solution(mesh):
    in_specs = (
        P("fsdp", "ctx", None),
        P("fsdp", None),
        P("fsdp", None),
        P("fsdp", None),
        P(),
        P("fsdp", "ctx"),
    )
    out_specs = P("fsdp", "ctx", None)
    return jax.shard_map(
        on_device, mesh=mesh, in_specs=in_specs, out_specs=out_specs, check_vma=False
    )
```

profile of v0, /device:TPU:0, one launch (start us, length us, event | category | flops | bytes accessed | tf_op | source)
XLA Modules:
  0.0 1176.6 jit_solution(5774909089922595813)
XLA Ops:
  7.3 2.8 reshape.460
  10.1 8.5 add_select_fusion.13
  18.6 5.6 pad_add_fusion
  24.2 28.0 %copy.44 = s32[32,64,320,4]{0,3,2,1:T(4,128)} copy(s32[32,64,320,4]{2,1,3,0:T(8,128)} %pad_add_fusion) | data formatting | bytes 20971520 | tf_op jit(solution)/shard_map/stack | solution.py:36
  52.4 151.2 %fusion.33 = bf16[32,81920]{0,1:T(8,128)(2,1)} fusion(s32[32,81920]{0,1:T(8,128)} %bitcast.50, f32[32,1280]{0,1:T(8,128)S(1)} %copy.45), kind=kLoop, calls=%fused_computation.65 | loop fusion | flops 243793920 | bytes 15892480 | tf_op jit(solution)/shard_map/convert_element_type | solution.py:54
  203.6 17.3 %copy.46 = bf16[32,81920]{1,0:T(8,128)(2,1)} copy(bf16[32,81920]{0,1:T(8,128)(2,1)} %fusion.33) | data formatting | bytes 10485760 | tf_op jit(solution)/shard_map/convert_element_type | solution.py:54
  221.7 4.3 reshape.463
  225.9 133.4 %all-gather.5.cloned.1.call-done = bf16[128,81920]{1,0:T(8,128)(2,1)} async-done(((bf16[32,81920]{1,0:T(8,128)(2,1)}), bf16[128,81920]{1,0:T(8,128)(2,1)}) %all-gather.5.cloned.1.call-update) | async-done | bytes 20971536 | tf_op jit(solution)/shard_map/all_gather | solution.py:98
  359.4 23.6 %reshape.462 = bf16[8192,1280]{1,0:T(8,128)(2,1)} reshape(bf16[128,81920]{1,0:T(8,128)(2,1)} %all-gather.5.cloned.1.call-done) | data formatting | bytes 41943040 | tf_op jit(solution)/shard_map/reshape | solution.py:102
  383.0 18.7 %fusion.41 = f32[512,1280]{0,1:T(8,128)} fusion(bf16[8192,1280]{1,0:T(8,128)(2,1)} %reshape.462, bf16[1,512,8192]{2,1,0:T(8,128)(2,1)} %param.12), kind=kOutput, calls=%fused_computation.96 | convolution fusion | flops 10737418240 | bytes 31981568 | tf_op jit(solution)/shard_map/dot_general | solution.py:101
  401.7 7.9 fusion.40
  411.0 80.8 %all-gather = s32[1,16384]{1,0:T(1,128)S(1)} all-gather(s32[1,512]{1,0:T(1,128)S(1)} %copy-done.2), channel_id=2, replica_groups=mesh['fsdp'=4,'ctx'=32] {'ctx'}, dimensions={1}, use_global_device_ids=true | all-gather | bytes 67584 | tf_op jit(solution)/shard_map/all_gather | solution.py:120
  497.8 78.2 %all-gather.9.cloned.1.call-done = bf16[16384,256]{0,1:T(8,128)(2,1)} async-done(((bf16[512,256]{0,1:T(8,128)(2,1)}), bf16[16384,256]{0,1:T(8,128)(2,1)}) %all-gather.9.cloned.1.call-update) | async-done | bytes 8388624 | tf_op jit(solution)/shard_map/all_gather | solution.py:130
  576.2 591.1 %while.21 = (s32[]{:T(128)}, f32[8,256]{1,0:T(8,128)S(1)}, f32[8,256]{1,0:T(8,128)S(1)}, f32[8,256,128]{2,1,0:T(8,128)S(1)}, f32[8,256]{1,0:T(8,128)S(1)}, /*ind...) while((s32[]{:T(128)}, f32[8,256]{1,0:T(8,128)S(1)}, ...), condition=%wide.region_12.13_spmd, body=%wide.region_2.0_spmd.sunk | while | flops 546447616 | bytes 19405304 | solution.py:151
  582.1 2.0 conditional.5
  585.4 2.0 conditional.4
  593.3 2.0 conditional.5
  602.5 2.0 conditional.5
  611.7 2.0 conditional.5
  620.9 2.0 conditional.5
  630.1 2.0 conditional.5
  639.3 2.0 conditional.5
  642.6 2.0 conditional.4
  657.7 2.0 conditional.5
  666.9 2.0 conditional.5
  676.1 2.0 conditional.5
  685.3 2.0 conditional.5
  694.5 2.0 conditional.5
  703.8 2.0 conditional.5
  713.0 2.0 conditional.5
  716.3 2.0 conditional.4
  731.4 2.0 conditional.5
  734.7 2.0 conditional.4
  749.8 2.0 conditional.5
  759.0 2.0 conditional.5
  768.2 2.0 conditional.5
  786.6 2.0 conditional.5
  805.0 2.0 conditional.5
  814.2 2.0 conditional.5
  823.4 2.0 conditional.5
  826.7 2.0 conditional.4
  841.8 2.0 conditional.5
  860.2 2.0 conditional.5
  878.6 2.0 conditional.5
  897.0 2.0 conditional.5
  915.5 2.0 conditional.5
  924.7 2.0 conditional.5
  933.9 2.0 conditional.5
  943.1 2.0 conditional.5
  952.3 2.0 conditional.5
  970.7 2.0 conditional.5
  989.1 2.0 conditional.5
  998.3 2.0 conditional.5
  1007.5 2.0 conditional.5
  1025.9 2.0 conditional.5
  1035.1 2.0 conditional.5
  1044.3 2.0 conditional.5
  1062.7 2.0 conditional.5
  1081.1 2.0 conditional.5
  1099.5 2.0 conditional.5
  1117.9 2.0 conditional.5
  1136.3 2.0 conditional.5
  1154.8 2.0 conditional.5
  1158.1 2.0 conditional.4
  (827 shorter events, 420.5 us)
Async XLA Ops:
  6.5 395.2 %copy-start = (bf16[64,1280]{1,0:T(8,128)(2,1)S(1)}, bf16[64,1280]{1,0:T(8,128)(2,1)}, u32[]{:S(2)}) copy-start(bf16[64,1280]{1,0:T(8,128)(2,1)} %param.16) | copy-start | bytes 491524
  6.5 215.1 %all-gather.7.cloned.1.call-start = ((), (), s32[]{:S(2)}) async-start(), calls=%async_computation.1 | async-start | bytes 1310720 | tf_op jit(solution)/shard_map/all_gather | solution.py:99
  7.3 352.1 %all-gather.5.cloned.1.call-start = ((), (), s32[]{:S(2)}) async-start(), calls=%async_computation | async-start | bytes 26214400 | tf_op jit(solution)/shard_map/all_gather | solution.py:98
  24.2 28.0 %copy-start.1 = (bf16[32,1280]{1,0:T(8,128)(2,1)S(1)}, bf16[32,1280]{1,0:T(8,128)(2,1)}, u32[]{:S(2)}) copy-start(bf16[32,1280]{1,0:T(8,128)(2,1)} %param.14) | copy-start | bytes 245764
  220.9 0.7 copy-start.2
  221.0 355.1 %all-gather.9.cloned.1.call-start = ((), (), s32[]{:S(2)}) async-start(), calls=%async_computation.2 | async-start | bytes 8650752 | tf_op jit(solution)/shard_map/all_gather | solution.py:130
Sparse Core Ops, SparseCore 0:
  9.0 23.3 all-gather.6
  221.1 138.2 all-gather.4
  411.1 164.9 all-gather.8
where the time goes:
time: 1180 us
  local copies, waits for them, and re-layouts  285 us (24%)
  other arithmetic  251 us (21%)
  loops' own time  213 us (18%)
  waiting for transfers between devices  212 us (18%)
  matrix products  121 us (10%)
  blocking collectives  80.8 us (7%)
  between operations  13.3 us (1%)
    another operation x1, loops' own time, on_device(): lax.scan(one_tile, states, jnp.arange(count // half_size, dtype=jnp.int32))  208 us
    dynamic_slice x128, local copies, waits for them, and re-layouts, one_tile(): tile = lax.dynamic_slice_in_dim(piece, tile_idx * half_size, half_size, 0)  164 us
    convert_element_type x1, other arithmetic, dequantize(): return scaled.reshape(-1, scaled.shape[-1]).astype(jnp.bfloat16)  151 us
    all_gather x1, waiting for transfers between devices, on_device(): weight_piece = lax.all_gather(own_weight, 'fsdp', axis=0, tiled=True)  133 us
    all_gather x1, blocking collectives, on_device(): all_positions = lax.all_gather(local_pos, 'ctx', axis=0, tiled=True)  80.8 us
    all_gather x1, waiting for transfers between devices, on_device(): piece = lax.all_gather(keys_values, 'ctx', axis=0, tiled=True)  78.2 us
    dot_general x65, matrix products, tile_update(): jnp.einsum('hqk,kd->hqd', weights, tile[:, HD:], preferred_element_type=j...  65.4 us
    reduce_min x64, other arithmetic, one_tile(): visible = jnp.min(tile_pos) <= jnp.max(pos_parts[part_idx])  49.6 us
  transfers between devices with their start and end apart: 3, of which 2 were waited for; matrix products, arithmetic and copies ran while one was open for 19% of the time, Pallas kernels for 0%

commit v1 on v0

v1 whole, which is shorter than its diff:
```python
import jax
import jax.numpy as jnp
from jax import lax
from jax.experimental import pallas as pl
from jax.experimental.pallas import tpu as pltpu
from jax.sharding import PartitionSpec as P

MESH = pl.DeviceIdType.MESH
QH = 8
HD = 128
HEADS = QH + 2
HALF = 256
TOK = 512
WIDTH = 8192
OUT = 1280
ROWS = 2048
RANK = 64
META = 16
PIECE = 512 + META
ROPE_BASE = 500000.0
LEVELS = (
    -1.0, -0.6961928009986877, -0.5250730514526367, -0.39491748809814453,
    -0.28444138169288635, -0.18477343022823334, -0.09105003625154495, 0.0,
    0.07958029955625534, 0.16093020141124725, 0.24611230194568634, 0.33791524171829224,
    0.44070982933044434, 0.5626170039176941, 0.7229568362236023, 1.0,
)
F32 = jnp.float32
BF16 = jnp.bfloat16
NT = (((1,), (1,)), ((), ()))
NEG = -1e30


def iota(shape, dim):
    return lax.broadcasted_iota(jnp.int32, shape, dim)


def head_order():
    p = iota((HD, HD), 1)
    return jnp.where(iota((HD, HD), 0) == 4 * (p % 32) + p // 32, 1.0, 0.0).astype(BF16)


def dequant_kernel(codes, scales, up, w_out, up_out, raw, nat, sc, sems):
    b = pl.program_id(0)

    def fetch(i):
        return pltpu.make_async_copy(codes.at[i // 8, :, i % 8, :], raw.at[i], sems.at[i])

    @pl.when(b == 0)
    def _():
        def start(i, carry):
            fetch(i).start()
            return carry

        lax.fori_loop(0, 32, start, 0)
        order = head_order()
        for h in range(HEADS):
            cols = slice(h * HD, (h + 1) * HD)
            sc[h] = jnp.dot(scales[:, cols], order, preferred_element_type=F32)
            up_out[:, cols] = jnp.dot(up[:, cols], order, preferred_element_type=F32).astype(BF16)

    fetch(b).wait()
    left = iota((8, 128), 1) < 64
    for g in range(4):
        u = [raw[b, pl.ds(40 * g + i, 8, stride=5), :] for i in range(5)]
        r2, r3, r4 = (pltpu.roll(u[i], 64, 1) for i in (2, 3, 4))
        for j in range(3):
            nat[j, pl.ds(16 * g, 8, stride=2), :] = u[j]
        odd = (jnp.where(left, r2, r3), jnp.where(left, r3, r4), r4)
        for j in range(3):
            nat[j, pl.ds(16 * g + 1, 8, stride=2), :] = odd[j]
    lane = iota((64, 128), 1)
    shift = 4 * (lane // 32)
    small = iota((64, 128), 1) % 16
    table = jnp.zeros((64, 128), F32)
    for n, level in enumerate(LEVELS):
        table = jnp.where(small == n, level, table)
    for h in range(HEADS):
        j, t = h // 4, h % 4
        words = nat[j]
        words = jnp.take_along_axis(words, lane % 32 + 32 * t, axis=1, mode="promise_in_bounds")
        code = (words >> shift) & 15
        level = jnp.take_along_axis(table, code, axis=1, mode="promise_in_bounds")
        cols = slice(h * HD, (h + 1) * HD)
        w_out[:, cols] = (level * sc[h, pl.ds(b, 1), :]).astype(BF16)


def dequant(codes, scales, up):
    view = codes.reshape(4, 8, 160, 128).transpose(0, 2, 1, 3)
    whole = lambda shape: pl.BlockSpec(shape, lambda b: (0, 0))
    return pl.pallas_call(
        dequant_kernel,
        grid=(32,),
        out_shape=(
            jax.ShapeDtypeStruct((ROWS, OUT), BF16),
            jax.ShapeDtypeStruct((RANK, OUT), BF16),
        ),
        in_specs=[pl.BlockSpec(memory_space=pl.ANY), whole((32, OUT)), whole((RANK, OUT))],
        out_specs=(pl.BlockSpec((64, OUT), lambda b: (b, 0)), whole((RANK, OUT))),
        scratch_shapes=[
            pltpu.VMEM((32, 160, 128), jnp.int32),
            pltpu.VMEM((3, 64, 128), jnp.int32),
            pltpu.VMEM((HEADS, 32, HD), F32),
            pltpu.SemaphoreType.DMA((32,)),
        ],
        compiler_params=pltpu.CompilerParams(vmem_limit_bytes=32 << 20),
        name="dequant",
    )(view, scales, up)


def place():
    f, c = lax.axis_index("fsdp"), lax.axis_index("ctx")
    return f // 2, f % 2, c // 16, (c // 4) % 4, c % 4


def device(z_hi, core, z_lo, x, y):
    return (z_hi * 2 + core, z_lo * 16 + (x % 4) * 4 + y % 4)


def project_kernel(
    pos, tok_hbm, w_hbm, d_hbm, up, q_out, kv_out,
    wbuf, dbuf, tok, acc, accd, cos_ref, sin_ref,
    local, wsend, wrecv, dsend, drecv,
):
    z_hi, core, z_lo, x, y = place()
    z = z_hi * 2 + z_lo
    cross_z = jnp.where(z % 2 == 0, (z + 3) % 4, (z + 1) % 4)
    cross = device(cross_z // 2, core, cross_z % 2, x, y)
    partner = device(z_hi, 1 - core, z_lo, x, y)
    xp, xm = device(z_hi, core, z_lo, x + 1, y), device(z_hi, core, z_lo, x + 3, y)
    yp, ym = device(z_hi, core, z_lo, x, y + 1), device(z_hi, core, z_lo, x, y + 3)
    col = (x + 2 * y) % 4

    tok_copy = pltpu.make_async_copy(tok_hbm, tok, local.at[0])
    own_w = pltpu.make_async_copy(w_hbm, wbuf.at[0], local.at[1])
    own_d = pltpu.make_async_copy(d_hbm, dbuf.at[0], local.at[2])
    own_w.start()
    own_d.start()
    tok_copy.start()

    barrier = pltpu.get_barrier_semaphore()
    for peer in (cross, partner, xp, xm, yp, ym):
        pl.semaphore_signal(barrier, inc=1, device_id=peer, device_id_type=MESH)
    pl.semaphore_wait(barrier, 6)

    shift = (0, 3, 1, 2)

    def rows_of(k, c):
        quarter = (col + shift[k]) % 4
        return pl.ds(pl.multiple_of(quarter * 512 + c * 128, 128), 128)

    def drows_of(k):
        quarter = (col + shift[k]) % 4
        return pl.ds(pl.multiple_of(quarter * 256, 256), 256)

    def wcopy(kind, c, src, dst, peer):
        return pltpu.make_async_remote_copy(
            src_ref=src, dst_ref=dst, send_sem=wsend.at[kind, c], recv_sem=wrecv.at[kind, c],
            device_id=peer, device_id_type=MESH,
        )

    def dcopy(kind, src, dst, peer):
        return pltpu.make_async_remote_copy(
            src_ref=src, dst_ref=dst, send_sem=dsend.at[kind], recv_sem=drecv.at[kind],
            device_id=peer, device_id_type=MESH,
        )

    def w_of(kind, c):
        if kind == 0:
            rows = rows_of(0, c)
            return wcopy(0, c, w_hbm.at[rows, :], wbuf.at[2, rows, :], cross)
        if kind in (1, 2, 3):
            rows = rows_of(0, c)
            peer = xp if kind == 1 else xm if kind == 2 else (yp, ym)[c % 2]
            return wcopy(kind, c, wbuf.at[2, rows, :], wbuf.at[2, rows, :], peer)
        if kind == 4:
            rows = pl.ds(c * 512, 512)
            return wcopy(4, c, w_hbm.at[rows, :], wbuf.at[1, rows, :], partner)
        rows = rows_of(kind - 5, c)
        return wcopy(kind, c, wbuf.at[2, rows, :], wbuf.at[3, rows, :], partner)

    def d_of(kind):
        if kind == 0:
            rows = drows_of(0)
            return dcopy(0, d_hbm.at[rows, :], dbuf.at[2, rows, :], cross)
        if kind in (1, 2, 3):
            rows = drows_of(0)
            return dcopy(kind, dbuf.at[2, rows, :], dbuf.at[2, rows, :], (xp, xm, yp)[kind - 1])
        if kind == 4:
            return dcopy(4, d_hbm, dbuf.at[1], partner)
        rows = drows_of(kind - 5)
        return dcopy(kind, dbuf.at[2, rows, :], dbuf.at[3, rows, :], partner)

    for c in range(4):
        w_of(0, c).start()
        if c == 0:
            d_of(0).start()
        w_of(4, c).start()
    d_of(4).start()

    half = HD // 2
    lane = iota((TOK, HD), 1)
    row = iota((TOK, HD), 0)
    index = (4 * (lane % 16) + lane // 32).astype(F32)
    inverse = jnp.exp(-jnp.log(F32(ROPE_BASE)) * 2.0 * index / HD)
    token_pos = jnp.where(row < HALF, row + pos[0, 0], row - HALF + pos[0, HALF])
    angle = token_pos.astype(F32) * inverse
    cos_ref[...] = jnp.cos(angle)
    sin_ref[...] = jnp.where(lane % 32 < 16, -1.0, 1.0) * jnp.sin(angle)

    acc[...] = jnp.zeros_like(acc)
    accd[...] = jnp.zeros_like(accd)
    tok_copy.wait()
    own_w.wait()
    own_d.wait()

    def arrive(c):
        w_of(0, c).wait_recv()
        for kind in (1, 2, 3, 5):
            w_of(kind, c).start()
        if c == 0:
            d_of(0).wait_recv()
            for kind in (1, 2, 3, 5):
                d_of(kind).start()

    def onward(c):
        for kind in (1, 2, 3):
            w_of(kind, c).wait_recv()
            w_of(5 + kind, c).start()
        if c == 0:
            for kind in (1, 2, 3):
                d_of(kind).wait_recv()
                d_of(5 + kind).start()

    def from_partner(kinds, cs):
        for kind in kinds:
            for c in cs:
                w_of(5 + kind, c).wait_recv()
            if 0 in cs:
                d_of(5 + kind).wait_recv()

    def events(u):
        def at(k):
            return pl.when(u == k)

        for k in range(4):
            @at(8 + 2 * k)
            def _():
                w_of(4, k).wait_recv()
                if k == 0:
                    d_of(4).wait_recv()

        @at(11)
        def _():
            arrive(0)

        @at(16)
        def _():
            arrive(1)

        @at(17)
        def _():
            onward(0)
            arrive(2)
            onward(1)

        @at(20)
        def _():
            from_partner((0,), (0, 1))

        @at(21)
        def _():
            from_partner((1, 2, 3), (0, 1))
            onward(2)
            arrive(3)

        @at(25)
        def _():
            onward(3)

        @at(28)
        def _():
            from_partner((0, 1, 2, 3), (2, 3))

    def unit(u, carry):
        events(u)
        late = u >= 16
        v = u % 8
        slot = jnp.where(late, 2 + (v // 4), u // 8)
        kind = v % 4
        moved = jnp.where(kind == 1, 3, jnp.where(kind == 2, 1, jnp.where(kind == 3, 2, 0)))
        quarter = jnp.where(late, (col + moved) % 4, v // 2)
        part = jnp.where(late, (u - 16) // 8, v % 2)
        base = quarter * 512 + part * 256
        other = 1 - z_hi
        owner = jnp.where(slot == 0, z_hi * 2 + core, jnp.where(
            slot == 1, z_hi * 2 + 1 - core, jnp.where(slot == 2, other * 2 + core, other * 2 + 1 - core)))
        t = tok[:, pl.ds(pl.multiple_of(owner * ROWS + base, 256), 256)]
        acc[...] += jnp.dot(
            t, wbuf[slot, pl.ds(pl.multiple_of(base, 256), 256), :], preferred_element_type=F32)
        accd[part] += jnp.dot(
            t, dbuf[slot, pl.ds(pl.multiple_of(quarter * 256, 256), 256), :], preferred_element_type=F32)
        return carry

    lax.fori_loop(0, 32, unit, 0)

    low = (accd[0] + pltpu.roll(accd[1], half, 1)).astype(BF16)[:, :RANK]
    start0, start1 = pos[0, 0], pos[0, HALF]
    swap = start0 > start1
    lower = jnp.where(swap, start1, start0)
    first = lane % 32 < 16
    eye = jnp.where(iota((HD, HD), 0) == iota((HD, HD), 1), 1.0, 0.0).astype(BF16)
    order = head_order()

    def joined(h):
        cols = slice(h * HD, (h + 1) * HD)
        return acc[:, cols] + 0.5 * jnp.dot(low, up[:, cols], preferred_element_type=F32)

    def rope(u):
        pair = jnp.where(first, pltpu.roll(u, HD - 16, 1), pltpu.roll(u, 16, 1))
        return u * cos_ref[...] + pair * sin_ref[...]

    def halves(a, axis):
        lo = lax.slice_in_dim(a, 0, HALF, axis=axis)
        hi = lax.slice_in_dim(a, HALF, TOK, axis=axis)
        return jnp.where(swap, hi, lo), jnp.where(swap, lo, hi)

    for h in range(QH):
        q = (rope(joined(h)) * HD ** (-0.5)).astype(BF16)
        qt = lax.dot_general(eye, q, NT, preferred_element_type=F32)
        for s, part in enumerate(halves(qt, 1)):
            q_out[s, :, h * HALF : (h + 1) * HALF] = part.astype(BF16)
    for s, part in enumerate(halves(rope(joined(QH)), 0)):
        kv_out[s, :HALF, :] = part.astype(BF16)
    v = joined(QH + 1).astype(BF16)
    vt = lax.dot_general(order, v, NT, preferred_element_type=F32)
    for s, part in enumerate(halves(vt, 1)):
        kv_out[s, HALF : HALF + 128, :] = part[:, :128].astype(BF16)
        kv_out[s, HALF + 128 : HALF + 256, :] = part[:, 128:].astype(BF16)
        kv_out[s, 2 * HALF :, :] = (jnp.zeros((META, HD), F32) + (lower // HALF).astype(F32)).astype(BF16)

    for c in range(4):
        for kind in range(9):
            w_of(kind, c).wait_send()
    for kind in range(9):
        d_of(kind).wait_send()


def project(pos, tokens, weight, down, up):
    anywhere = pl.BlockSpec(memory_space=pl.ANY)
    vmem = pl.BlockSpec(memory_space=pltpu.VMEM)
    dma = pltpu.SemaphoreType.DMA
    return pl.pallas_call(
        project_kernel,
        out_shape=(
            jax.ShapeDtypeStruct((2, HD, QH * HALF), BF16),
            jax.ShapeDtypeStruct((2, PIECE, HD), BF16),
        ),
        in_specs=[pl.BlockSpec(memory_space=pltpu.SMEM), anywhere, anywhere, anywhere, vmem],
        out_specs=(vmem, vmem),
        scratch_shapes=[
            pltpu.VMEM((4, ROWS, OUT), BF16),
            pltpu.VMEM((4, ROWS // 2, HD), BF16),
            pltpu.VMEM((TOK, WIDTH), BF16),
            pltpu.VMEM((TOK, OUT), F32),
            pltpu.VMEM((2, TOK, HD), F32),
            pltpu.VMEM((TOK, HD), F32),
            pltpu.VMEM((TOK, HD), F32),
            dma((3,)), dma((9, 4)), dma((9, 4)), dma((9,)), dma((9,)),
        ],
        compiler_params=pltpu.CompilerParams(
            collective_id=0, has_side_effects=True, vmem_limit_bytes=60 << 20),
        name="project",
    )(pos, tokens, weight, down, up)


ORDER = (
    (0, 0, 0), (0, 1, 0), (0, 3, 0), (0, 0, 1), (0, 0, 3), (1, 0, 0), (0, 2, 0), (0, 0, 2),
    (0, 1, 3), (0, 1, 1), (0, 3, 3), (1, 1, 0), (0, 3, 1), (1, 3, 0), (0, 2, 1), (1, 0, 1),
    (0, 2, 3), (0, 1, 2), (1, 0, 3), (1, 3, 1), (1, 1, 1), (0, 3, 2), (1, 3, 3), (1, 1, 3),
    (1, 2, 0), (1, 2, 1), (0, 2, 2), (1, 0, 2), (1, 2, 3), (1, 3, 2), (1, 1, 2), (1, 2, 2),
)
SLOT = {s: i for i, s in enumerate(ORDER)}
BLOCKS = len(ORDER)
AHEAD = 1


def routes():
    table = {}
    for p in (0, 1):
        table[(0, 1, 0), p] = ("xp", (0, 0, 0))
        table[(0, 3, 0), p] = ("xm", (0, 0, 0))
        for dx in range(4):
            table[(0, dx, 1), p] = ("yp", (0, dx, 0))
            table[(0, dx, 3), p] = ("ym", (0, dx, 0))
        for s in ((0, 0), (1, 0), (3, 0), (2, 0), (0, 1), (0, 3)):
            table[(1,) + s, p] = ("z", (0,) + s)
        for dy in (1, 2, 3):
            table[(1, 1, dy), p] = ("xp", (1, 0, dy))
            table[(1, 3, dy), p] = ("xm", (1, 0, dy))
    table[(0, 2, 0), 0] = ("xm", (0, 3, 0))
    table[(0, 2, 0), 1] = ("xp", (0, 1, 0))
    for dx in range(4):
        table[(0, dx, 2), 0] = ("ym", (0, dx, 3))
        table[(0, dx, 2), 1] = ("yp", (0, dx, 1))
    table[(1, 0, 2), 0] = ("ym", (1, 0, 3))
    table[(1, 0, 2), 1] = ("yp", (1, 0, 1))
    for dy in (1, 2, 3):
        table[(1, 2, dy), 0] = ("xm", (1, 3, dy))
        table[(1, 2, dy), 1] = ("xp", (1, 1, dy))
    return table


def forwards():
    opposite = {"xp": "xm", "xm": "xp", "yp": "ym", "ym": "yp", "z": "z"}
    table = {i: [] for i in range(BLOCKS)}
    for (s, p), (origin, source) in routes().items():
        table[SLOT[source]].append((SLOT[s], p, opposite[origin]))
    return {i: sorted(v) for i, v in table.items()}


def attend_kernel(pos, q, kv, out, kvbuf, k2, vt1, vt2, m_ref, acc, local, send, recv):
    z_hi, core, z_lo, x, y = place()
    peers = {
        "xp": device(z_hi, core, z_lo, x + 1, y), "xm": device(z_hi, core, z_lo, x + 3, y),
        "yp": device(z_hi, core, z_lo, x, y + 1), "ym": device(z_hi, core, z_lo, x, y + 3),
        "z": device(z_hi, core, 1 - z_lo, x, y),
    }
    table = forwards()
    own = pltpu.make_async_copy(kv, kvbuf.at[0], local.at[0])
    own.start()
    barrier = pltpu.get_barrier_semaphore()
    for peer in peers.values():
        pl.semaphore_signal(barrier, inc=1, device_id=peer, device_id_type=MESH)
    pl.semaphore_wait(barrier, len(peers))
    own.wait()

    def copy(source, slot, piece, peer):
        return pltpu.make_async_remote_copy(
            src_ref=kvbuf.at[source, piece], dst_ref=kvbuf.at[slot, piece],
            send_sem=send.at[slot, piece], recv_sem=recv.at[slot, piece],
            device_id=peer, device_id_type=MESH,
        )

    def forward(source):
        for slot, piece, to in table[source]:
            copy(source, slot, piece, peers[to]).start()

    def take(slot):
        for piece in range(2):
            copy(0, slot, piece, peers["z"]).wait_recv()

    forward(0)

    start0, start1 = pos[0, 0], pos[0, HALF]
    swap = start0 > start1
    mine = (jnp.where(swap, start1, start0) // HALF).astype(F32)
    vt1[HD:, :] = jnp.ones((META, HALF), BF16)
    vt2[HD:, :] = jnp.ones((META, HALF), BF16)

    def keys(slot, piece):
        return kvbuf[slot, piece, :HALF, :]

    def values(slot, piece):
        return jnp.concatenate(
            [kvbuf[slot, piece, HALF : HALF + 128, :], kvbuf[slot, piece, HALF + 128 : HALF + 256, :]], axis=1)

    def scores(k, qt):
        return jnp.dot(k, qt, preferred_element_type=F32)

    def weigh(vt, s, m):
        return jnp.dot(vt, jnp.exp(s - m).astype(BF16), preferred_element_type=F32)

    def top(s):
        return jnp.max(s, axis=0, keepdims=True)

    vt1[:HD, :] = values(0, 0)
    vt2[:HD, :] = values(0, 1)
    k2[...] = keys(0, 1)

    def own_head(h, carry):
        cols = pl.ds(pl.multiple_of(h * HALF, HALF), HALF)
        q0, q1 = q[0, :, cols], q[1, :, cols]
        seen = iota((HALF, HALF), 0) <= iota((HALF, HALF), 1)
        s00 = jnp.where(seen, scores(keys(0, 0), q0), -jnp.inf)
        m0 = top(s00)
        m_ref[0, h] = jnp.broadcast_to(m0, (8, HALF))
        acc[0, h] = weigh(vt1[...], s00, m0)
        s10 = scores(keys(0, 0), q1)
        s11 = jnp.where(seen, scores(k2[...], q1), -jnp.inf)
        m1 = jnp.maximum(top(s10), top(s11))
        m_ref[1, h] = jnp.broadcast_to(m1, (8, HALF))
        acc[1, h] = weigh(vt1[...], s10, m1) + weigh(vt2[...], s11, m1)
        return carry

    lax.fori_loop(0, QH, own_head, 0)

    def step(i, carry):
        for k in range(1, BLOCKS):
            if table[k]:
                @pl.when(i + AHEAD == k)
                def _():
                    take(k)
                    forward(k)
            else:
                @pl.when(i + AHEAD == k)
                def _():
                    take(k)

        @pl.when(i > 0)
        def _():
            theirs = jnp.max(kvbuf[i, 0, 2 * HALF :, :].astype(F32))
            c = theirs < mine
            lo_bias = jnp.where(c, 0.0, NEG)
            hi_bias = jnp.where(c, NEG, 0.0)
            w_lo = jnp.where(c, 1.0, 0.0)
            w_hi = jnp.where(c, 0.0, 1.0)
            k2[...] = jnp.where(c, keys(i, 0), keys(i, 1))
            vt1[:HD, :] = values(i, 0)
            vt2[:HD, :] = jnp.where(c, values(i, 0), values(i, 1))

            def head(h, carry):
                cols = pl.ds(pl.multiple_of(h * HALF, HALF), HALF)
                q1 = q[1, :, cols]
                q2 = jnp.where(c, q[0, :, cols], q1)
                s1 = scores(keys(i, 0), q1)
                s2 = scores(k2[...], q2)
                t1, t2 = top(s1), top(s2)
                m_lo, m_hi = m_ref[0, h, :1, :], m_ref[1, h, :1, :]
                n_lo = jnp.maximum(m_lo, t2 + lo_bias)
                n_hi = jnp.maximum(m_hi, jnp.maximum(t1, t2 + hi_bias))
                o1 = weigh(vt1[...], s1, n_hi)
                o2 = weigh(vt2[...], s2, jnp.where(c, n_lo, n_hi))
                f_lo, f_hi = jnp.exp(m_lo - n_lo), jnp.exp(m_hi - n_hi)
                m_ref[0, h] = jnp.broadcast_to(n_lo, (8, HALF))
                m_ref[1, h] = jnp.broadcast_to(n_hi, (8, HALF))
                acc[0, h] = acc[0, h] * f_lo + o2 * w_lo
                acc[1, h] = acc[1, h] * f_hi + (o1 + o2 * w_hi)
                return carry

            lax.fori_loop(0, QH, head, 0)

        return carry

    lax.fori_loop(1 - AHEAD, BLOCKS, step, 0)

    for h in range(QH):
        cols = slice(h * HD, (h + 1) * HD)
        parts = []
        for s in range(2):
            total = acc[s, h, HD : HD + 1, :]
            parts.append((acc[s, h, :HD, :] / total).T)
        out[:HALF, cols] = jnp.where(swap, parts[1], parts[0]).astype(BF16)
        out[HALF:, cols] = jnp.where(swap, parts[0], parts[1]).astype(BF16)

    def drain(slot, carry):
        for piece in range(2):
            copy(0, slot, piece, peers["z"]).wait_send()
        return carry

    lax.fori_loop(1, BLOCKS, drain, 0)


def attend(pos, q, kv):
    anywhere = pl.BlockSpec(memory_space=pl.ANY)
    vmem = pl.BlockSpec(memory_space=pltpu.VMEM)
    dma = pltpu.SemaphoreType.DMA
    return pl.pallas_call(
        attend_kernel,
        out_shape=jax.ShapeDtypeStruct((TOK, QH * HD), BF16),
        in_specs=[pl.BlockSpec(memory_space=pltpu.SMEM), vmem, anywhere],
        out_specs=vmem,
        scratch_shapes=[
            pltpu.VMEM((BLOCKS, 2, PIECE, HD), BF16),
            pltpu.VMEM((HALF, HD), BF16),
            pltpu.VMEM((HD + META, HALF), BF16),
            pltpu.VMEM((HD + META, HALF), BF16),
            pltpu.VMEM((2, QH, 8, HALF), F32),
            pltpu.VMEM((2, QH, HD + META, HALF), F32),
            dma((1,)), dma((BLOCKS, 2)), dma((BLOCKS, 2)),
        ],
        compiler_params=pltpu.CompilerParams(
            collective_id=1, has_side_effects=True, vmem_limit_bytes=60 << 20),
        name="attend",
    )(pos, q, kv)


def on_device(tokens, codes, scales, down_adapter_matrix, up_adapter_matrix, positions):
    weight, up = dequant(codes, scales, up_adapter_matrix)
    down = down_adapter_matrix.reshape(4, 2, HALF, RANK).transpose(0, 2, 1, 3).reshape(ROWS // 2, HD)
    q, kv = project(positions, tokens[0], weight, down, up)
    return attend(positions, q, kv)[None]


def solution(mesh):
    return jax.shard_map(
        on_device,
        mesh=mesh,
        in_specs=(
            P("fsdp", "ctx", None), P("fsdp", None), P("fsdp", None), P("fsdp", None), P(), P("fsdp", "ctx"),
        ),
        out_specs=P("fsdp", "ctx", None),
        check_vma=False,
    )
```

time: 1180 us -> 244 us (0.21)
  local copies, waits for them, and re-layouts: 285 us -> 11.7 us
  other arithmetic: 251 us -> 0 us
  Pallas kernels: 0 us -> 232 us
  loops' own time: 213 us -> 0 us
  waiting for transfers between devices: 212 us -> 0 us
  matrix products: 121 us -> 0 us
  blocking collectives: 80.8 us -> 0 us
  between operations: 13.3 us -> 0.05 us
    pallas_call x0 -> x3, Pallas kernels: none -> 232 us  [the longest x1 150 us: attend(): pl.pallas_call(attend_kernel, out_shape=jax.ShapeDtypeStruct((TOK, QH * H...]
    another operation x129 -> x0, loops' own time: 213 us -> none  [the longest x1 208 us: on_device(): lax.scan(one_tile, states, jnp.arange(count // half_size, dtype=jnp.int32))]
    all_gather x3 -> x0, waiting for transfers between devices: 212 us -> none  [the longest x1 133 us: on_device(): weight_piece = lax.all_gather(own_weight, 'fsdp', axis=0, tiled=True)]
    dynamic_slice x192 -> x0, local copies, waits for them, and re-layouts: 202 us -> none  [the longest x128 164 us: one_tile(): tile = lax.dynamic_slice_in_dim(piece, tile_idx * half_size, half_size, 0)]
    convert_element_type x4 -> x0, other arithmetic: 152 us -> none  [the longest x1 151 us: dequantize(): return scaled.reshape(-1, scaled.shape[-1]).astype(jnp.bfloat16)]
    dot_general x132 -> x0, matrix products: 121 us -> none  [the longest x65 65.4 us: tile_update(): jnp.einsum('hqk,kd->hqd', weights, tile[:, HD:], preferred_element_type=j...]
    all_gather x1 -> x0, blocking collectives: 80.8 us -> none  [on_device(): all_positions = lax.all_gather(local_pos, 'ctx', axis=0, tiled=True)]
    reduce_min x64 -> x0, other arithmetic: 49.6 us -> none  [one_tile(): visible = jnp.min(tile_pos) <= jnp.max(pos_parts[part_idx])]
  transfers between devices with their start and end apart: 3 -> 0, of which waited for: 2 -> 0; matrix products, arithmetic and copies ran while one was open for 19% -> 0% of each run, Pallas kernels for 0% -> 0%
where the time goes in v1:
time: 244 us
  Pallas kernels  232 us (95%)
  local copies, waits for them, and re-layouts  11.7 us (5%)
    pallas_call x1, Pallas kernels, attend(): pl.pallas_call(attend_kernel, out_shape=jax.ShapeDtypeStruct((TOK, QH * H...  150 us
    pallas_call x1, Pallas kernels, project(): pl.pallas_call(project_kernel, out_shape=(jax.ShapeDtypeStruct((2, HD, QH...  60.8 us
    pallas_call x1, Pallas kernels, dequant(): pl.pallas_call(dequant_kernel, grid=(32,), out_shape=(jax.ShapeDtypeStruc...  21.6 us
    unnamed x11, local copies, waits for them, and re-layouts  8.77 us

profile of v1, /device:TPU:0, one launch (start us, length us, event | category | flops | bytes accessed | tf_op | source)
XLA Modules:
  0.0 243.8 jit_solution(2093759109728517420)
XLA Ops:
  0.0 1.5 reshape.10
  1.5 0.5 copy.10
  2.0 1.0 reshape.12.d_hbm
  3.0 0.0 copy-start.1
  3.0 1.7 copy-done.1
  4.7 0.0 copy-start.2
  4.7 0.9 copy-done.2
  5.6 0.0 copy-start.4
  5.6 0.9 copy-done.4
  6.5 21.6 %dequant.1 = (bf16[2048,1280]{1,0:T(8,128)(2,1)S(1)}, bf16[64,1280]{1,0:T(8,128)(2,1)S(1)}) custom-call(s32[4,160,8,128]{3,2,1,0:T(8,128)S(1)} %bitcast.6, bf16[32,1280]{1,0:T(8,128)(2,1)S(1)} %copy-done.4, bf16[64,1280]{1,0:T(8,128)(2,1)S(1)} %copy-done.2), custom_call_target="tpu_custom_call" | custom-call | tf_op jit(solution)/shard_map/dequant/pallas_call | solution.py:90
  28.1 0.0 copy-start
  28.1 2.3 copy-done
  30.4 0.0 copy-start.3
  30.4 0.7 copy-done.3
  31.1 60.8 %project.1 = (bf16[2,128,2048]{2,1,0:T(8,128)(2,1)}, bf16[2,528,128]{2,1,0:T(8,128)(2,1)}) custom-call(s32[1,512]{1,0:T(1,128)} %pos.3, bf16[512,8192]{1,0:T(8,128)(2,1)} %bitcast.7, bf16[2048,1280]{1,0:T(8,128)(2,1)} %copy-done, bf16[1024,128]{1,0:T(8,128)(2,1)} %reshape.12.d_hbm, bf16[64,1280]{1,0:T(8,128)(2,1)} %copy-done.3), custom_call_target="tpu_custom_call" | custom-call | tf_op jit(solution)/shard_map/project/pallas_call | solution.py:352
  91.9 149.7 %attend.1 = bf16[512,1024]{1,0:T(8,128)(2,1)} custom-call(s32[1,512]{1,0:T(1,128)} %pos.3, bf16[2,128,2048]{2,1,0:T(8,128)(2,1)} %get-tuple-element.11.q, bf16[2,528,128]{2,1,0:T(8,128)(2,1)} %get-tuple-element.12.kv), custom_call_target="tpu_custom_call" | custom-call | tf_op jit(solution)/shard_map/attend/pallas_call | solution.py:567
  241.6 2.3 copy.13
Async XLA Ops:
  3.0 1.7 copy-start.1
  4.7 0.9 copy-start.2
  5.6 0.9 copy-start.4
  28.1 2.3 copy-start
  30.4 0.7 copy-start.3

commit v2 on v1

v2 whole, which is shorter than its diff:
```python
import jax
import jax.numpy as jnp
from jax import lax
from jax.experimental import pallas as pl
from jax.experimental.pallas import tpu as pltpu
from jax.sharding import PartitionSpec as P

MESH = pl.DeviceIdType.MESH
QH = 8
HD = 128
HEADS = QH + 2
HALF = 256
TOK = 512
WIDTH = 8192
OUT = 1280
ROWS = 2048
RANK = 64
META = 16
PIECE = 512 + META
ROPE_BASE = 500000.0
LEVELS = (
    -1.0, -0.6961928009986877, -0.5250730514526367, -0.39491748809814453,
    -0.28444138169288635, -0.18477343022823334, -0.09105003625154495, 0.0,
    0.07958029955625534, 0.16093020141124725, 0.24611230194568634, 0.33791524171829224,
    0.44070982933044434, 0.5626170039176941, 0.7229568362236023, 1.0,
)
F32 = jnp.float32
BF16 = jnp.bfloat16
NT = (((1,), (1,)), ((), ()))
NEG = -1e30
LOG2E = 1.4426950408889634


def iota(shape, dim):
    return lax.broadcasted_iota(jnp.int32, shape, dim)


def head_order():
    p = iota((HD, HD), 1)
    return jnp.where(iota((HD, HD), 0) == 4 * (p % 32) + p // 32, 1.0, 0.0).astype(BF16)


def plane(t):
    depth = 512 if t < 8 else 256
    lane = iota((depth, HD), 1)
    column = 4 * lane + t % 4 if t < 8 else 4 * (lane % 64) + 2 * (t - 8) + lane // 64
    return (t // 4) * 512, jnp.where(iota((depth, HD), 0) == column, 1.0, 0.0).astype(BF16)


def lookup(tables, words, move):
    numbers = lax.GatherDimensionNumbers(
        offset_dims=(), collapsed_slice_dims=(0,), start_index_map=(0,),
        operand_batching_dims=(1,), start_indices_batching_dims=(1,))
    index = (words >> move) & 7
    low, high = (
        lax.gather(t, index[..., None], numbers, slice_sizes=(1, 1), mode=lax.GatherScatterMode.PROMISE_IN_BOUNDS)
        for t in tables)
    return jnp.where((words & (8 << move)) != 0, high, low)


def place():
    f, c = lax.axis_index("fsdp"), lax.axis_index("ctx")
    return f // 2, f % 2, c // 16, (c // 4) % 4, c % 4


def device(z_hi, core, z_lo, x, y):
    return (z_hi * 2 + core, z_lo * 16 + (x % 4) * 4 + y % 4)


def project_kernel(
    pos, tok_hbm, codes, scales, d_hbm, up_in, q_out, kv_out,
    wbuf, dbuf, tok, acc, accd, cos_ref, sin_ref, raw, nat, sc, up,
    local, fetched, wsend, wrecv, dsend, drecv,
):
    z_hi, core, z_lo, x, y = place()
    z = z_hi * 2 + z_lo
    cross_z = jnp.where(z % 2 == 0, (z + 3) % 4, (z + 1) % 4)
    cross = device(cross_z // 2, core, cross_z % 2, x, y)
    partner = device(z_hi, 1 - core, z_lo, x, y)
    xp, xm = device(z_hi, core, z_lo, x + 1, y), device(z_hi, core, z_lo, x + 3, y)
    yp, ym = device(z_hi, core, z_lo, x, y + 1), device(z_hi, core, z_lo, x, y + 3)
    col = (x + 2 * y) % 4

    def block(n):
        return (col * 8 + n) % 32

    def fetch(n):
        b = block(n)
        return pltpu.make_async_copy(codes.at[b // 8, :, b % 8, :], raw.at[b], fetched.at[n])

    def start(n, carry):
        fetch(n).start()
        return carry

    lax.fori_loop(0, 32, start, 0)
    tok_copy = pltpu.make_async_copy(tok_hbm, tok, local.at[0])
    own_d = pltpu.make_async_copy(d_hbm, dbuf.at[0], local.at[1])
    own_d.start()
    tok_copy.start()

    barrier = pltpu.get_barrier_semaphore()
    for peer in (cross, partner, xp, xm, yp, ym):
        pl.semaphore_signal(barrier, inc=1, device_id=peer, device_id_type=MESH)

    for t in range(HEADS):
        first, picks = plane(t)
        cols = slice(first, first + picks.shape[0])
        sc[t] = jnp.dot(scales[:, cols], picks, preferred_element_type=F32)
        half_up = 0.5 * jnp.dot(up_in[:, cols], picks, preferred_element_type=F32)
        up[:, t * HD : (t + 1) * HD] = half_up.astype(BF16)
    pl.semaphore_wait(barrier, 6)

    shift = (0, 3, 1, 2)

    def rows_of(k, c):
        quarter = (col + shift[k]) % 4
        return pl.ds(pl.multiple_of(quarter * 512 + c * 128, 128), 128)

    def drows_of(k):
        quarter = (col + shift[k]) % 4
        return pl.ds(pl.multiple_of(quarter * 256, 256), 256)

    def wcopy(kind, c, src, dst, peer):
        return pltpu.make_async_remote_copy(
            src_ref=src, dst_ref=dst, send_sem=wsend.at[kind, c], recv_sem=wrecv.at[kind, c],
            device_id=peer, device_id_type=MESH,
        )

    def dcopy(kind, src, dst, peer):
        return pltpu.make_async_remote_copy(
            src_ref=src, dst_ref=dst, send_sem=dsend.at[kind], recv_sem=drecv.at[kind],
            device_id=peer, device_id_type=MESH,
        )

    def w_of(kind, c):
        if kind == 0:
            rows = rows_of(0, c)
            return wcopy(0, c, wbuf.at[0, rows, :], wbuf.at[2, rows, :], cross)
        if kind in (1, 2, 3):
            rows = rows_of(0, c)
            peer = xp if kind == 1 else xm if kind == 2 else (yp, ym)[c % 2]
            return wcopy(kind, c, wbuf.at[2, rows, :], wbuf.at[2, rows, :], peer)
        if kind == 4:
            rows = pl.ds(pl.multiple_of((col + c) % 4 * 512, 512), 512)
            return wcopy(4, c, wbuf.at[0, rows, :], wbuf.at[1, rows, :], partner)
        rows = rows_of(kind - 5, c)
        return wcopy(kind, c, wbuf.at[2, rows, :], wbuf.at[3, rows, :], partner)

    def d_of(kind):
        if kind == 0:
            rows = drows_of(0)
            return dcopy(0, d_hbm.at[rows, :], dbuf.at[2, rows, :], cross)
        if kind in (1, 2, 3):
            rows = drows_of(0)
            return dcopy(kind, dbuf.at[2, rows, :], dbuf.at[2, rows, :], (xp, xm, yp)[kind - 1])
        if kind == 4:
            return dcopy(4, d_hbm, dbuf.at[1], partner)
        rows = drows_of(kind - 5)
        return dcopy(kind, dbuf.at[2, rows, :], dbuf.at[3, rows, :], partner)

    d_of(0).start()
    d_of(4).start()

    left = iota((8, HD), 1) < 64
    place_in = iota((64, HD), 1)
    digit = 4 * (place_in // 64)
    tables = []
    for first in (0, 8):
        table = jnp.zeros((8, HD), F32)
        for n in range(8):
            table = jnp.where(iota((8, HD), 0) == n, LEVELS[first + n], table)
        tables.append(table)

    def dequantize(n, slot):
        b = block(n)
        fetch(n).wait()
        for g in range(4):
            u = [raw[b, pl.ds(40 * g + i, 8, stride=5), :] for i in range(5)]
            r2, r3, r4 = (pltpu.roll(u[i], 64, 1) for i in (2, 3, 4))
            odd = (jnp.where(left, r2, r3), jnp.where(left, r3, r4), r4)
            for j in range(3):
                nat[slot, j, pl.ds(16 * g, 8, stride=2), :] = u[j]
                nat[slot, j, pl.ds(16 * g + 1, 8, stride=2), :] = odd[j]

    def levels(n, slot):
        b = block(n)
        rows = pl.ds(pl.multiple_of(b * 64, 64), 64)
        for t in range(HEADS):
            words = nat[slot, t // 4]
            if t < 8:
                move = 4 * (t % 4)
            else:
                words = jnp.where(place_in < 64, words, pltpu.roll(words, 64, 1))
                move = digit + 8 * (t - 8)
            level = jnp.concatenate(
                [lookup(tables, words[r : r + 8], move if t < 8 else move[:8]) for r in range(0, 64, 8)], axis=0)
            wbuf[0, rows, t * HD : (t + 1) * HD] = (level * sc[t, pl.ds(b, 1), :]).astype(BF16)

    def pair(n, carry):
        dequantize(2 * n, 0)
        dequantize(2 * n + 1, 1)
        levels(2 * n, 0)
        levels(2 * n + 1, 1)

        @pl.when(n <= 4)
        def _():
            for c in range(4):
                @pl.when(n == c + 1)
                def _():
                    w_of(0, c).start()

        @pl.when((n > 0) & (n % 4 == 0))
        def _():
            for c in range(3):
                @pl.when(n == 4 * c + 4)
                def _():
                    w_of(4, c).start()

        return carry

    lax.fori_loop(0, 16, pair, 0)

    row = iota((64, TOK), 0)
    lane = iota((64, TOK), 1)
    index = (4 * (row % 16) + row // 16).astype(F32)
    inverse = jnp.exp(-jnp.log(F32(ROPE_BASE)) * 2.0 * index / HD)
    token_pos = jnp.where(lane < HALF, lane + pos[0, 0], lane - HALF + pos[0, HALF])
    angle = token_pos.astype(F32) * inverse
    cos_ref[...] = jnp.cos(angle)
    sin_ref[...] = jnp.sin(angle)

    w_of(4, 3).start()
    acc[...] = jnp.zeros_like(acc)
    accd[...] = jnp.zeros_like(accd)
    tok_copy.wait()
    own_d.wait()

    def arrive(c):
        w_of(0, c).wait_recv()
        for kind in (1, 2, 3, 5):
            w_of(kind, c).start()
        if c == 0:
            d_of(0).wait_recv()
            for kind in (1, 2, 3, 5):
                d_of(kind).start()

    def onward(c):
        for kind in (1, 2, 3):
            w_of(kind, c).wait_recv()
            w_of(5 + kind, c).start()
        if c == 0:
            for kind in (1, 2, 3):
                d_of(kind).wait_recv()
                d_of(5 + kind).start()

    def from_partner(kinds, cs):
        for kind in kinds:
            for c in cs:
                w_of(5 + kind, c).wait_recv()
            if 0 in cs:
                d_of(5 + kind).wait_recv()

    def early(u, carry):
        @pl.when(u == 0)
        def _():
            arrive(0)

        @pl.when(u == 4)
        def _():
            arrive(1)
            onward(0)
            d_of(4).wait_recv()

        for k in range(4):
            @pl.when(u == 4 + k)
            def _():
                w_of(4, k).wait_recv()

        slot = u // 4
        quarter = (col + u % 4) % 4
        base = quarter * 512
        owner = z_hi * 2 + jnp.where(slot == 0, core, 1 - core)
        t = tok[:, pl.ds(pl.multiple_of(owner * ROWS + base, 512), 512)]
        acc[...] += jnp.dot(
            t, wbuf[slot, pl.ds(pl.multiple_of(base, 512), 512), :], preferred_element_type=F32)
        d = dbuf[slot, pl.ds(pl.multiple_of(quarter * 256, 256), 256), :]
        for part in range(2):
            accd[part] += jnp.dot(t[:, part * 256 : part * 256 + 256], d, preferred_element_type=F32)
        return carry

    lax.fori_loop(0, 8, early, 0)
    arrive(2)
    onward(1)

    def late(u, carry):
        @pl.when(u == 4)
        def _():
            from_partner((0, 1, 2, 3), (0, 1))
            arrive(3)

        @pl.when(u == 7)
        def _():
            onward(2)

        @pl.when(u == 9)
        def _():
            from_partner((0,), (2, 3))

        @pl.when(u == 10)
        def _():
            onward(3)

        @pl.when(u == 13)
        def _():
            from_partner((1, 2, 3), (2, 3))

        part = u // 8
        v = u % 8
        slot = jnp.where(part == 0, 2 + v // 4, jnp.where(v < 2, 2 + v, 2 + (v - 2) // 3))
        kind = jnp.where(part == 0, v % 4, jnp.where(v < 2, 0, 1 + (v - 2) % 3))
        moved = jnp.where(kind == 1, 3, jnp.where(kind == 2, 1, jnp.where(kind == 3, 2, 0)))
        quarter = (col + moved) % 4
        base = quarter * 512 + part * 256
        owner = (1 - z_hi) * 2 + jnp.where(slot == 2, core, 1 - core)
        t = tok[:, pl.ds(pl.multiple_of(owner * ROWS + base, 256), 256)]
        acc[...] += jnp.dot(
            t, wbuf[slot, pl.ds(pl.multiple_of(base, 256), 256), :], preferred_element_type=F32)
        accd[part] += jnp.dot(
            t, dbuf[slot, pl.ds(pl.multiple_of(quarter * 256, 256), 256), :], preferred_element_type=F32)
        return carry

    lax.fori_loop(0, 16, late, 0)

    low = (accd[0] + pltpu.roll(accd[1], 64, 1)).astype(BF16)[:, :RANK]
    start0, start1 = pos[0, 0], pos[0, HALF]
    swap = start0 > start1
    lower = jnp.where(swap, start1, start0)
    pair = jnp.where(iota((HD, 2 * HD), 0) == iota((HD, 2 * HD), 1) % HD, 1.0, 0.0).astype(BF16)

    def joined(t):
        cols = slice(t * HD, (t + 1) * HD)
        full = acc[:, cols] + jnp.dot(low, up[:, cols], preferred_element_type=F32)
        high = full.astype(BF16)
        rest = (full - high.astype(F32)).astype(BF16)
        return lax.dot_general(pair, jnp.concatenate([high, rest], axis=1), NT, preferred_element_type=F32)

    def rope(u, k):
        c, n = cos_ref[16 * k : 16 * k + 16, :], sin_ref[16 * k : 16 * k + 16, :]
        return jnp.concatenate([u[:16] * c - u[16:] * n, u[16:] * c + u[:16] * n], axis=0)

    def halves(a, axis):
        lo = lax.slice_in_dim(a, 0, HALF, axis=axis)
        hi = lax.slice_in_dim(a, HALF, TOK, axis=axis)
        return jnp.where(swap, hi, lo), jnp.where(swap, lo, hi)

    ahead = joined(0)
    for j in range(2):
        for k in range(4):
            turned = ahead
            ahead = joined(4 * j + k + 1)
            for t in range(4):
                q = (rope(turned[32 * t : 32 * t + 32], k) * HD ** (-0.5)).astype(BF16).astype(F32) * LOG2E
                cols = slice((4 * j + t) * HALF, (4 * j + t + 1) * HALF)
                for s, part in enumerate(halves(q, 1)):
                    high = part.astype(BF16)
                    q_out[s, 32 * k : 32 * k + 32, cols] = high
                    q_out[s, HD + 32 * k : HD + 32 * k + 32, cols] = (part - high.astype(F32)).astype(BF16)
    both = (ahead, joined(9))
    key = jnp.concatenate(
        [rope(both[k // 2][64 * (k % 2) : 64 * (k % 2) + 32], k) for k in range(4)], axis=0)
    for s, part in enumerate(halves(key.T, 0)):
        kv_out[s, :HALF, :] = part.astype(BF16)
    value = jnp.concatenate(
        [both[k // 2][64 * (k % 2) + 32 : 64 * (k % 2) + 64] for k in range(4)], axis=0).astype(BF16)
    vt = jnp.dot(head_order(), value, preferred_element_type=F32)
    for s, part in enumerate(halves(vt, 1)):
        kv_out[s, HALF : HALF + 128, :] = part[:, :128].astype(BF16)
        kv_out[s, HALF + 128 : HALF + 256, :] = part[:, 128:].astype(BF16)
        kv_out[s, 2 * HALF :, :] = (jnp.zeros((META, HD), F32) + (lower // HALF).astype(F32)).astype(BF16)

    for c in range(4):
        for kind in range(9):
            w_of(kind, c).wait_send()
    for kind in range(9):
        d_of(kind).wait_send()


def project(pos, tokens, codes, scales, down, up):
    view = codes.reshape(4, 8, 160, HD).transpose(0, 2, 1, 3)
    anywhere = pl.BlockSpec(memory_space=pl.ANY)
    vmem = pl.BlockSpec(memory_space=pltpu.VMEM)
    dma = pltpu.SemaphoreType.DMA
    return pl.pallas_call(
        project_kernel,
        out_shape=(
            jax.ShapeDtypeStruct((2, 2 * HD, QH * HALF), BF16),
            jax.ShapeDtypeStruct((2, PIECE, HD), BF16),
        ),
        in_specs=[pl.BlockSpec(memory_space=pltpu.SMEM), anywhere, anywhere, vmem, anywhere, vmem],
        out_specs=(vmem, vmem),
        scratch_shapes=[
            pltpu.VMEM((4, ROWS, OUT), BF16),
            pltpu.VMEM((4, ROWS // 2, HD), BF16),
            pltpu.VMEM((TOK, WIDTH), BF16),
            pltpu.VMEM((TOK, OUT), F32),
            pltpu.VMEM((2, TOK, HD), F32),
            pltpu.VMEM((64, TOK), F32),
            pltpu.VMEM((64, TOK), F32),
            pltpu.VMEM((32, 160, HD), jnp.int32),
            pltpu.VMEM((2, 3, 64, HD), jnp.int32),
            pltpu.VMEM((HEADS, 32, HD), F32),
            pltpu.VMEM((RANK, OUT), BF16),
            dma((2,)), dma((32,)), dma((9, 4)), dma((9, 4)), dma((9,)), dma((9,)),
        ],
        compiler_params=pltpu.CompilerParams(
            collective_id=0, has_side_effects=True, vmem_limit_bytes=60 << 20),
        name="project",
    )(pos, tokens, view, scales, down, up)


ORDER = (
    (0, 0, 0), (0, 1, 0), (0, 3, 0), (0, 0, 1), (0, 0, 3), (1, 0, 0), (0, 2, 0), (0, 0, 2),
    (0, 1, 3), (0, 1, 1), (0, 3, 3), (1, 1, 0), (0, 3, 1), (1, 3, 0), (0, 2, 1), (1, 0, 1),
    (0, 2, 3), (0, 1, 2), (1, 0, 3), (1, 3, 1), (1, 1, 1), (0, 3, 2), (1, 3, 3), (1, 1, 3),
    (1, 2, 0), (1, 2, 1), (0, 2, 2), (1, 0, 2), (1, 2, 3), (1, 3, 2), (1, 1, 2), (1, 2, 2),
)
SLOT = {s: i for i, s in enumerate(ORDER)}
BLOCKS = len(ORDER)
AHEAD = 1


def routes():
    table = {}
    for p in (0, 1):
        table[(0, 1, 0), p] = ("xp", (0, 0, 0))
        table[(0, 3, 0), p] = ("xm", (0, 0, 0))
        for dx in range(4):
            table[(0, dx, 1), p] = ("yp", (0, dx, 0))
            table[(0, dx, 3), p] = ("ym", (0, dx, 0))
        for s in ((0, 0), (1, 0), (3, 0), (2, 0), (0, 1), (0, 3)):
            table[(1,) + s, p] = ("z", (0,) + s)
        for dy in (1, 2, 3):
            table[(1, 1, dy), p] = ("xp", (1, 0, dy))
            table[(1, 3, dy), p] = ("xm", (1, 0, dy))
    table[(0, 2, 0), 0] = ("xm", (0, 3, 0))
    table[(0, 2, 0), 1] = ("xp", (0, 1, 0))
    for dx in range(4):
        table[(0, dx, 2), 0] = ("ym", (0, dx, 3))
        table[(0, dx, 2), 1] = ("yp", (0, dx, 1))
    table[(1, 0, 2), 0] = ("ym", (1, 0, 3))
    table[(1, 0, 2), 1] = ("yp", (1, 0, 1))
    for dy in (1, 2, 3):
        table[(1, 2, dy), 0] = ("xm", (1, 3, dy))
        table[(1, 2, dy), 1] = ("xp", (1, 1, dy))
    return table


def forwards():
    opposite = {"xp": "xm", "xm": "xp", "yp": "ym", "ym": "yp", "z": "z"}
    table = {i: [] for i in range(BLOCKS)}
    for (s, p), (origin, source) in routes().items():
        table[SLOT[source]].append((SLOT[s], p, opposite[origin]))
    return {i: sorted(v) for i, v in table.items()}


def attend_kernel(pos, q, kv, out, kvbuf, k2, vt1, vt2, m_ref, acc, local, send, recv):
    z_hi, core, z_lo, x, y = place()
    peers = {
        "xp": device(z_hi, core, z_lo, x + 1, y), "xm": device(z_hi, core, z_lo, x + 3, y),
        "yp": device(z_hi, core, z_lo, x, y + 1), "ym": device(z_hi, core, z_lo, x, y + 3),
        "z": device(z_hi, core, 1 - z_lo, x, y),
    }
    table = forwards()
    own = pltpu.make_async_copy(kv, kvbuf.at[0], local.at[0])
    own.start()
    barrier = pltpu.get_barrier_semaphore()
    for peer in peers.values():
        pl.semaphore_signal(barrier, inc=1, device_id=peer, device_id_type=MESH)
    pl.semaphore_wait(barrier, len(peers))
    own.wait()

    def copy(source, slot, piece, peer):
        return pltpu.make_async_remote_copy(
            src_ref=kvbuf.at[source, piece], dst_ref=kvbuf.at[slot, piece],
            send_sem=send.at[slot, piece], recv_sem=recv.at[slot, piece],
            device_id=peer, device_id_type=MESH,
        )

    def forward(source):
        for slot, piece, to in table[source]:
            copy(source, slot, piece, peers[to]).start()

    def take(slot):
        for piece in range(2):
            copy(0, slot, piece, peers["z"]).wait_recv()

    forward(0)

    start0, start1 = pos[0, 0], pos[0, HALF]
    swap = start0 > start1
    mine = (jnp.where(swap, start1, start0) // HALF).astype(F32)
    one = jnp.ones((META, HALF), BF16)
    vt1[HD:, :HALF] = one
    vt2[HD:, :] = one

    def keys(slot, piece):
        return kvbuf[slot, piece, :HALF, :]

    def values(slot, piece):
        return jnp.concatenate(
            [kvbuf[slot, piece, HALF : HALF + 128, :], kvbuf[slot, piece, HALF + 128 : HALF + 256, :]], axis=1)

    def scores(k, qt):
        return jnp.dot(jnp.concatenate([k, k], axis=1), qt, preferred_element_type=F32)

    def weigh(vt, s, m):
        return jnp.dot(vt, jnp.exp2(s - m).astype(BF16), preferred_element_type=F32)

    def top(s):
        return jnp.max(s, axis=0, keepdims=True)

    vt1[:HD, :HALF] = values(0, 0)
    vt2[:HD, :] = values(0, 1)
    k2[...] = keys(0, 1)

    def own_head(h, carry):
        cols = pl.ds(pl.multiple_of(h * HALF, HALF), HALF)
        q0, q1 = q[0, :, cols], q[1, :, cols]
        seen = iota((HALF, HALF), 0) <= iota((HALF, HALF), 1)
        s00 = jnp.where(seen, scores(keys(0, 0), q0), -jnp.inf)
        m0 = top(s00)
        m_ref[0, h] = jnp.broadcast_to(m0, (8, HALF))
        acc[0, h] = weigh(vt1[:, :HALF], s00, m0)
        s10 = scores(keys(0, 0), q1)
        s11 = jnp.where(seen, scores(k2[...], q1), -jnp.inf)
        m1 = jnp.maximum(top(s10), top(s11))
        m_ref[1, h] = jnp.broadcast_to(m1, (8, HALF))
        acc[1, h] = weigh(vt1[:, :HALF], s10, m1) + weigh(vt2[...], s11, m1)
        return carry

    lax.fori_loop(0, QH, own_head, 0, unroll=2)

    def step(i, carry):
        def come(k):
            @pl.when(i + AHEAD == k)
            def _():
                take(k)
                forward(k)

        for group in range(0, BLOCKS, 6):
            @pl.when((i + AHEAD >= group) & (i + AHEAD < group + 6))
            def _():
                for k in range(max(group, 1), min(group + 6, BLOCKS)):
                    come(k)

        @pl.when(i > 0)
        def _():
            theirs = jnp.max(kvbuf[i, 0, 2 * HALF :, :].astype(F32))
            c = theirs < mine
            lo_bias = jnp.where(c, 0.0, NEG)
            hi_bias = jnp.where(c, NEG, 0.0)
            w_lo = jnp.where(c, 1.0, 0.0)
            w_hi = jnp.where(c, 0.0, 1.0)
            k2[...] = jnp.where(c, keys(i, 0), keys(i, 1))
            vt1[:HD, :HALF] = values(i, 0)
            low_v, zero = values(i, 0), jnp.zeros((HD, HALF), BF16)
            vt1[:HD, HALF:] = jnp.where(c, zero, values(i, 1))
            vt1[HD:, HALF:] = jnp.where(c, zero[:META], one)
            vt2[:HD, :] = jnp.where(c, low_v, zero)
            vt2[HD:, :] = jnp.where(c, one, zero[:META])

            def product(h):
                cols = slice(h * HALF, (h + 1) * HALF)
                q1 = q[1, :, cols]
                q2 = jnp.where(c, q[0, :, cols], q1)
                return scores(keys(i, 0), q1), scores(k2[...], q2)

            def soften(h, s1, s2):
                t1, t2 = top(s1), top(s2)
                m_lo, m_hi = m_ref[0, h, :1, :], m_ref[1, h, :1, :]
                n_lo = jnp.maximum(m_lo, t2 + lo_bias)
                n_hi = jnp.maximum(m_hi, jnp.maximum(t1, t2 + hi_bias))
                e1 = jnp.exp2(s1 - n_hi).astype(BF16)
                e2 = jnp.exp2(s2 - jnp.where(c, n_lo, n_hi)).astype(BF16)
                m_ref[0, h] = jnp.broadcast_to(n_lo, (8, HALF))
                m_ref[1, h] = jnp.broadcast_to(n_hi, (8, HALF))
                return e1, e2, jnp.exp2(m_lo - n_lo), jnp.exp2(m_hi - n_hi)

            def gather(h, e1, e2, f_lo, f_hi):
                o_hi = jnp.dot(vt1[...], jnp.concatenate([e1, e2], axis=0), preferred_element_type=F32)
                o_lo = jnp.dot(vt2[...], e2, preferred_element_type=F32)
                acc[0, h] = acc[0, h] * f_lo + o_lo
                acc[1, h] = acc[1, h] * f_hi + o_hi

            ahead, ready = product(0), None
            for h in range(QH):
                now = ahead
                if h + 1 < QH:
                    ahead = product(h + 1)
                if ready is not None:
                    gather(h - 1, *ready)
                ready = soften(h, *now)
            gather(QH - 1, *ready)

        return carry

    lax.fori_loop(1 - AHEAD, BLOCKS, step, 0)

    for h in range(QH):
        cols = slice(h * HD, (h + 1) * HD)
        parts = []
        for s in range(2):
            total = acc[s, h, HD : HD + 1, :]
            parts.append((acc[s, h, :HD, :] / total).T)
        out[:HALF, cols] = jnp.where(swap, parts[1], parts[0]).astype(BF16)
        out[HALF:, cols] = jnp.where(swap, parts[0], parts[1]).astype(BF16)

    def drain(slot, carry):
        for piece in range(2):
            copy(0, slot, piece, peers["z"]).wait_send()
        return carry

    lax.fori_loop(1, BLOCKS, drain, 0)


def attend(pos, q, kv):
    anywhere = pl.BlockSpec(memory_space=pl.ANY)
    vmem = pl.BlockSpec(memory_space=pltpu.VMEM)
    dma = pltpu.SemaphoreType.DMA
    return pl.pallas_call(
        attend_kernel,
        out_shape=jax.ShapeDtypeStruct((TOK, QH * HD), BF16),
        in_specs=[pl.BlockSpec(memory_space=pltpu.SMEM), vmem, anywhere],
        out_specs=vmem,
        scratch_shapes=[
            pltpu.VMEM((BLOCKS, 2, PIECE, HD), BF16),
            pltpu.VMEM((HALF, HD), BF16),
            pltpu.VMEM((HD + META, 2 * HALF), BF16),
            pltpu.VMEM((HD + META, HALF), BF16),
            pltpu.VMEM((2, QH, 8, HALF), F32),
            pltpu.VMEM((2, QH, HD + META, HALF), F32),
            dma((1,)), dma((BLOCKS, 2)), dma((BLOCKS, 2)),
        ],
        compiler_params=pltpu.CompilerParams(
            collective_id=1, has_side_effects=True, vmem_limit_bytes=60 << 20),
        name="attend",
    )(pos, q, kv)


def on_device(tokens, codes, scales, down_adapter_matrix, up_adapter_matrix, positions):
    down = down_adapter_matrix.reshape(4, 2, HALF, RANK).transpose(0, 2, 1, 3).reshape(ROWS // 2, HD)
    q, kv = project(positions, tokens[0], codes, scales, down, up_adapter_matrix)
    return attend(positions, q, kv)[None]


def solution(mesh):
    return jax.shard_map(
        on_device,
        mesh=mesh,
        in_specs=(
            P("fsdp", "ctx", None), P("fsdp", None), P("fsdp", None), P("fsdp", None), P(), P("fsdp", "ctx"),
        ),
        out_specs=P("fsdp", "ctx", None),
        check_vma=False,
    )
```

time: 244 us -> 151 us (0.62)
  Pallas kernels: 232 us -> 145 us
  local copies, waits for them, and re-layouts: 11.7 us -> 5.23 us
    pallas_call x1, Pallas kernels: 150 us -> 84.8 us  [attend(): pl.pallas_call(attend_kernel, out_shape=jax.ShapeDtypeStruct((TOK, QH * H...]
    pallas_call x2 -> x1, Pallas kernels: 82.4 us -> 59.8 us  [project(): pl.pallas_call(project_kernel, out_shape=(jax.ShapeDtypeStruct((2, 2 * HD...]
    unnamed x11 -> x1, local copies, waits for them, and re-layouts: 8.77 us -> 2.26 us
where the time goes in v2:
time: 151 us; the launch traced here: 150 us
  Pallas kernels  145 us (96%)
  local copies, waits for them, and re-layouts  5.23 us (3%)
    pallas_call x1, Pallas kernels, attend(): pl.pallas_call(attend_kernel, out_shape=jax.ShapeDtypeStruct((TOK, QH * H...  84.8 us
    pallas_call x1, Pallas kernels, project(): pl.pallas_call(project_kernel, out_shape=(jax.ShapeDtypeStruct((2, 2 * HD...  59.8 us

profile of v2, /device:TPU:0, one launch (start us, length us, event | category | flops | bytes accessed | tf_op | source)
XLA Modules:
  0.0 149.8 jit_solution(7736193620258749795)
XLA Ops:
  0.0 1.5 reshape.10
  1.5 0.5 copy.10
  2.0 1.0 reshape.12.d_hbm
  3.0 59.8 %project.1 = (bf16[2,256,2048]{2,1,0:T(8,128)(2,1)}, bf16[2,528,128]{2,1,0:T(8,128)(2,1)}) custom-call(s32[1,512]{1,0:T(1,128)} %pos.3, bf16[512,8192]{1,0:T(8,128)(2,1)} %bitcast.6, s32[4,160,8,128]{3,2,1,0:T(8,128)} %bitcast.8, bf16[32,1280]{1,0:T(8,128)(2,1)} %scales.1, bf16[1024,128]{1,0:T(8,128)(2,1)} %reshape.12.d_hbm, bf16[64,1280]{1,0:T(8,128)(2,1)} %up_in.1), custom_call_target="tpu_custom_call" | custom-call | tf_op jit(solution)/shard_map/project/pallas_call | solution.py:393
  62.8 84.8 %attend.1 = bf16[512,1024]{1,0:T(8,128)(2,1)} custom-call(s32[1,512]{1,0:T(1,128)} %pos.3, bf16[2,256,2048]{2,1,0:T(8,128)(2,1)} %get-tuple-element.7.q, bf16[2,528,128]{2,1,0:T(8,128)(2,1)} %get-tuple-element.8.kv), custom_call_target="tpu_custom_call" | custom-call | tf_op jit(solution)/shard_map/attend/pallas_call | solution.py:630
  147.6 2.3 %copy.13 = bf16[1,512,1024]{2,1,0:T(8,128)(2,1)} copy(bf16[1,512,1024]{2,1,0:T(8,128)(2,1)} %bitcast.7) | data formatting | bytes 2097152
